TPU v7x, 32 devices: a whole 2x2x4 slice. The times are simulated.
32 devices in a mesh: date: 2 (over y), row: 16 (over z, x, core).
Axes of the slice: x: 2, y: 2, z: 4, core: 2. Of those that a mesh axis runs over, the one named last changes fastest.
Arguments:
- slc: float32 [2, 128, 128, 256], P(None, 'date', 'row'), may hold values from -40 to 40, as said below
- network: int32 [128, 8], replicated, may hold values 0 or 1
Outputs:
- linked: float32 [2, 128, 128, 256], P(None, None, 'row', 'date')
Inputs may be any that keep to these rules, and one draw needn't show every extreme that they name: slc holds real and imaginary parts of complex samples.
All inputs are finite; a program needn't handle non-finite values.
Results may differ from a plain program's by a relative error of at most 0.0003.
Values sent between devices are 32-bit elements; how exact they have to be, the bound alone decides.
A program may use at most 192 MiB of HBM per device.

v0:
```python
import jax
import jax.numpy as jnp
from jax import lax
from jax.sharding import PartitionSpec as P

LOOK = 5
ITERS = 5


def extended_2(cells, sides, width):
    for axis, dim in sides:
        count = lax.axis_size(axis)
        ends = count - 1
        head = lax.slice_in_dim(cells, 0, width, axis=dim)
        tail = lax.slice_in_dim(cells, cells.shape[dim] - width, cells.shape[dim], axis=dim)
        cells = jnp.concatenate(
            [
                lax.ppermute(tail, axis, [(i, (i + 1) % count) for i in range(ends)]),
                cells,
                lax.ppermute(head, axis, [((i + 1) % count, i) for i in range(ends)]),
            ],
            axis=dim,
        )
    return cells


def band_table(count_out):
    count_in = count_out + 2 * LOOK
    outer = jnp.arange(count_out, dtype=jnp.int32)[:, None]
    inner = jnp.arange(count_in, dtype=jnp.int32)[None, :]
    reach = inner - outer
    return ((reach >= 0) & (reach <= 2 * LOOK)).astype(jnp.float32)


def box_sum(samples):
    rows_out = samples.shape[-2] - 2 * LOOK
    cols_out = samples.shape[-1] - 2 * LOOK
    row_table = band_table(rows_out)
    col_table = band_table(cols_out)
    total = jnp.einsum("...rc,kr->...kc", samples, row_table, precision=lax.Precision.HIGHEST)
    return jnp.einsum("...kc,mc->...km", total, col_table, precision=lax.Precision.HIGHEST)


def coherence(extended, network):
    num_dates = extended.shape[1]
    squares = extended[0] * extended[0] + extended[1] * extended[1]
    inverse_root = lax.rsqrt(box_sum(squares) + 1e-06)
    layers = []
    for offset in range(1, network.shape[1] + 1):
        earlier = extended[:, : num_dates - offset]
        later = extended[:, offset:]
        prod_re = earlier[0] * later[0] + earlier[1] * later[1]
        prod_im = earlier[1] * later[0] - earlier[0] * later[1]
        sums = box_sum(jnp.stack([prod_re, prod_im]))
        weight = network[: num_dates - offset, offset - 1].astype(jnp.float32)[:, None, None]
        weight = weight * inverse_root[: num_dates - offset] * inverse_root[offset:]
        layer = sums * weight[None]
        layers.append(jnp.pad(layer, ((0, 0), (0, offset), (0, 0), (0, 0))))
    return jnp.stack(layers)


def apply_matrix(coherent, vector):
    num_dates = vector.shape[1]
    image_re = vector[0]
    image_im = vector[1]
    for offset in range(1, coherent.shape[0] + 1):
        coh_re = coherent[offset - 1, 0]
        coh_im = coherent[offset - 1, 1]
        ahead = jnp.pad(vector[:, offset:], ((0, 0), (0, offset), (0, 0), (0, 0)))
        image_re = image_re + coh_re * ahead[0] - coh_im * ahead[1]
        image_im = image_im + coh_re * ahead[1] + coh_im * ahead[0]
        back_re = coh_re * vector[0] + coh_im * vector[1]
        back_im = coh_re * vector[1] - coh_im * vector[0]
        image_re = image_re + jnp.pad(back_re[: num_dates - offset], ((offset, 0), (0, 0), (0, 0)))
        image_im = image_im + jnp.pad(back_im[: num_dates - offset], ((offset, 0), (0, 0), (0, 0)))
    image = jnp.stack([image_re, image_im])
    meansq = jnp.mean(image[0] * image[0] + image[1] * image[1], axis=0)
    return image * lax.rsqrt(meansq + 1e-06)[None, None]


def power_iterate(coherent):
    start = jnp.stack([jnp.ones_like(coherent[0, 0]), jnp.zeros_like(coherent[0, 0])])

    def iterate_once(index, vector):
        return apply_matrix(coherent, vector)

    return lax.fori_loop(0, ITERS, iterate_once, start)


def regroup(samples):
    return lax.all_to_all(samples, "date", split_axis=3, concat_axis=1, tiled=True)


def add_row_rims(samples):
    return extended_2(samples, (("row", 2),), LOOK)


def add_column_rims(samples):
    return extended_2(samples, (("date", 3),), LOOK)


def on_device(slc, network):
    extended = add_column_rims(regroup(add_row_rims(slc)))
    coherent = coherence(extended, network)
    return power_iterate(coherent)


def solution(mesh):
    return jax.shard_map(
        on_device,
        mesh=mesh,
        in_specs=(P(None, "date", "row", None), P()),
        out_specs=P(None, None, "row", "date"),
        check_vma=False,
    )
```

profile of v0, /device:TPU:10, one launch (start us, length us, event | category | flops | bytes accessed | tf_op | source)
XLA Modules:
  0.0 409.5 jit_solution(18203681720282301117)
XLA Ops:
  10.9 11.1 %collective-permute-done = f32[2,64,5,256]{3,1,2,0:T(8,128)} collective-permute-done((f32[2,64,5,256]{3,1,2,0:T(8,128)}, f32[2,64,5,256]{3,1,2,0:T(8,128)}, u32[]{:S(2)}, u32[]{:S(2)}) %collective-permute-start) | collective-permute-done | bytes 655392 | tf_op jit(solution)/shard_map/ppermute | solution.py:18
  45.6 23.0 %all-to-all-done = f32[2,1,294912]{2,1,0:T(1,128)S(1)} async-done(((f32[2,1,294912]{2,1,0:T(1,128)}), f32[2,1,294912]{2,1,0:T(1,128)S(1)}, u32[]{:S(2)}, u32[]{:S(2)}) %all-to-all-start) | async-done | bytes 2359328 | tf_op jit(solution)/shard_map/all_to_all | solution.py:91
  69.1 9.0 %reduce = f32[2,294912]{1,0:T(2,128)} reduce(f32[2,1,294912]{2,1,0:T(1,128)S(1)} %all-to-all-done, f32[]{:T(128)} %broadcast.224), dimensions={1}, to_apply=%all_to_all.13.reduce_sub_computation | reduce | bytes 4718596 | tf_op jit(solution)/shard_map/all_to_all | solution.py:91
  78.1 7.5 %reshape.71 = f32[256,2,18,64]{3,2,1,0:T(8,128)} reshape(f32[2,294912]{1,0:T(2,128)} %reduce) | data formatting | bytes 4718592
  85.7 6.4 %copy.100 = f32[2,64,18,2,128]{4,3,1,2,0:T(2,128)} copy(f32[2,64,18,2,128]{1,2,0,4,3:T(8,128)} %bitcast.423) | data formatting | bytes 4718592 | tf_op jit(solution)/shard_map/all_to_all | solution.py:91
  121.5 6.4 %multiply_add_fusion.8 = (f32[1,120,18,138]{1,0,3,2:T(1,128)}, f32[1,120,18,138]{1,0,3,2:T(1,128)}) fusion(f32[2,128,18,138]{1,0,3,2:T(2,128)S(1)} %pad_maximum_fusion.1), kind=kLoop, calls=%fused_computation.112 | loop fusion | flops 1788480 | bytes 7153920 | tf_op jit(solution)/shard_map/add | solution.py:52
  127.8 6.4 %multiply_add_fusion.11 = (f32[1,123,18,138]{1,0,3,2:T(1,128)}, f32[1,123,18,138]{1,0,3,2:T(1,128)}) fusion(f32[2,128,18,138]{1,0,3,2:T(2,128)S(1)} %pad_maximum_fusion.1), kind=kLoop, calls=%fused_computation.118 | loop fusion | flops 1833192 | bytes 7332768 | tf_op jit(solution)/shard_map/add | solution.py:52
  134.2 6.4 %multiply_add_fusion.10 = (f32[1,122,18,138]{1,0,3,2:T(1,128)}, f32[1,122,18,138]{1,0,3,2:T(1,128)}) fusion(f32[2,128,18,138]{1,0,3,2:T(2,128)S(1)} %pad_maximum_fusion.1), kind=kLoop, calls=%fused_computation.116 | loop fusion | flops 1818288 | bytes 7273152 | tf_op jit(solution)/shard_map/add | solution.py:52
  140.6 6.6 %multiply_add_fusion.13 = (f32[1,125,18,138]{1,0,3,2:T(1,128)}, f32[1,125,18,138]{1,0,3,2:T(1,128)}) fusion(f32[2,128,18,138]{1,0,3,2:T(2,128)S(1)} %pad_maximum_fusion.1), kind=kLoop, calls=%fused_computation.122 | loop fusion | flops 1863000 | bytes 7452000 | tf_op jit(solution)/shard_map/add | solution.py:52
  147.2 6.4 %multiply_add_fusion.12 = (f32[1,124,18,138]{1,0,3,2:T(1,128)}, f32[1,124,18,138]{1,0,3,2:T(1,128)}) fusion(f32[2,128,18,138]{1,0,3,2:T(2,128)S(1)} %pad_maximum_fusion.1), kind=kLoop, calls=%fused_computation.120 | loop fusion | flops 1848096 | bytes 7392384 | tf_op jit(solution)/shard_map/add | solution.py:52
  153.6 6.5 %multiply_add_fusion.15 = (f32[1,127,18,138]{1,0,3,2:T(1,128)}, f32[1,127,18,138]{1,0,3,2:T(1,128)}) fusion(f32[2,128,18,138]{1,0,3,2:T(2,128)S(1)} %pad_maximum_fusion.1), kind=kLoop, calls=%fused_computation.126 | loop fusion | flops 1892808 | bytes 7571232 | tf_op jit(solution)/shard_map/add | solution.py:52
  160.1 6.4 %multiply_add_fusion.14 = (f32[1,126,18,138]{1,0,3,2:T(1,128)}, f32[1,126,18,138]{1,0,3,2:T(1,128)}) fusion(f32[2,128,18,138]{1,0,3,2:T(2,128)S(1)} %pad_maximum_fusion.1), kind=kLoop, calls=%fused_computation.124 | loop fusion | flops 1877904 | bytes 7511616 | tf_op jit(solution)/shard_map/add | solution.py:52
  169.3 6.7 %copy.94 = f32[2,121,18,138]{3,2,1,0:T(8,128)} copy(f32[2,121,18,138]{1,0,3,2:T(2,128)S(1)} %pad_maximum_fusion.8) | data formatting | bytes 4809024 | tf_op jit(solution)/shard_map/stack | solution.py:54
  176.0 6.2 %fusion.91 = f32[8,2,121,138]{3,0,2,1:T(8,128)} fusion(f32[2,121,18,138]{3,2,1,0:T(8,128)} %copy.94), kind=kOutput, calls=%fused_computation.174 | convolution fusion | flops 57708864 | bytes 3473184 | tf_op jit(solution)/shard_map/...rc,kr->...kc/dot_general | solution.py:40
  188.1 6.3 %copy.96 = f32[2,120,18,138]{3,2,1,0:T(8,128)} copy(f32[2,120,18,138]{1,0,3,2:T(2,128)S(1)} %pad_maximum_fusion.9) | data formatting | bytes 4769280 | tf_op jit(solution)/shard_map/stack | solution.py:54
  204.7 6.3 %copy.90 = f32[2,123,18,138]{3,2,1,0:T(8,128)} copy(f32[2,123,18,138]{1,0,3,2:T(2,128)S(1)} %pad_maximum_fusion.6) | data formatting | bytes 4888512 | tf_op jit(solution)/shard_map/stack | solution.py:54
  221.8 6.5 %copy.92 = f32[2,122,18,138]{3,2,1,0:T(8,128)} copy(f32[2,122,18,138]{1,0,3,2:T(2,128)S(1)} %pad_maximum_fusion.7) | data formatting | bytes 4848768 | tf_op jit(solution)/shard_map/stack | solution.py:54
  239.0 6.3 %copy.86 = f32[2,125,18,138]{3,2,1,0:T(8,128)} copy(f32[2,125,18,138]{1,0,3,2:T(2,128)S(1)} %pad_maximum_fusion.4) | data formatting | bytes 4968000 | tf_op jit(solution)/shard_map/stack | solution.py:54
  245.3 6.2 %fusion.99 = f32[8,2,125,138]{3,0,2,1:T(8,128)} fusion(f32[2,125,18,138]{3,2,1,0:T(8,128)} %copy.86), kind=kOutput, calls=%fused_computation.182 | convolution fusion | flops 59616576 | bytes 3588000 | tf_op jit(solution)/shard_map/...rc,kr->...kc/dot_general | solution.py:40
  256.2 6.8 %copy.88 = f32[2,124,18,138]{3,2,1,0:T(8,128)} copy(f32[2,124,18,138]{1,0,3,2:T(2,128)S(1)} %pad_maximum_fusion.5) | data formatting | bytes 4928256 | tf_op jit(solution)/shard_map/stack | solution.py:54
  273.9 6.3 %copy.80 = f32[2,127,18,138]{3,2,1,0:T(8,128)} copy(f32[2,127,18,138]{1,0,3,2:T(2,128)S(1)} %pad_maximum_fusion.2) | data formatting | bytes 5047488 | tf_op jit(solution)/shard_map/stack | solution.py:54
  280.2 6.3 %fusion.103 = f32[8,2,127,138]{3,0,2,1:T(8,128)} fusion(f32[2,127,18,138]{3,2,1,0:T(8,128)} %copy.80), kind=kOutput, calls=%fused_computation.186 | convolution fusion | flops 60570432 | bytes 3645408 | tf_op jit(solution)/shard_map/...rc,kr->...kc/dot_general | solution.py:40
  291.3 6.5 %copy.84 = f32[2,126,18,138]{3,2,1,0:T(8,128)} copy(f32[2,126,18,138]{1,0,3,2:T(2,128)S(1)} %pad_maximum_fusion.3) | data formatting | bytes 5007744 | tf_op jit(solution)/shard_map/stack | solution.py:54
  322.6 85.7 %while.12 = (s32[]{:T(128)}, f32[2,128,8,128]{3,2,1,0:T(8,128)S(1)}, f32[1,2,128,8,128]{4,3,2,1,0:T(8,128)}, f32[1,2,128,8,128]{4,3,2,1,0:T(8,128)}, f32[1,2,128...) while((s32[]{:T(128)}, ...), condition=%wide.region_2.3_spmd, body=%wide.region_0.2_spmd.sunk | while | flops 17605632 | bytes 115360056 | solution.py:87
  (333 shorter events, 235.5 us)
Async XLA Ops:
  1.7 7.7 %copy-start.8 = (f32[2,64,8,256]{3,2,1,0:T(8,128)S(1)}, f32[2,64,8,256]{3,2,1,0:T(8,128)}, u32[]{:S(2)}) copy-start(f32[2,64,8,256]{3,2,1,0:T(8,128)} %param.4) | copy-start | bytes 3145732
  2.8 19.2 %collective-permute-start = (f32[2,64,5,256]{3,1,2,0:T(8,128)}, f32[2,64,5,256]{3,1,2,0:T(8,128)}, u32[]{:S(2)}, u32[]{:S(2)}) collective-permute-start(f32[2,64,5,256]{3,1,2,0:T(8,128)} %copy.102), channel_id=1, source_target_pairs={{0,1},{1,2},{2,3},{3,4},{4,5},{5,6},{6,7},{7,8},{8,9},{9,10},{10,1... | collective-permute-start | bytes 1966088 | tf_op jit(solution)/shard_map/ppermute | solution.py:18
  4.7 6.2 %copy-start.39 = (s32[128,8]{0,1:T(8,128)S(1)}, s32[128,8]{0,1:T(8,128)}, u32[]{:S(2)}) copy-start(s32[128,8]{0,1:T(8,128)} %param.5) | copy-start | bytes 12292
  5.8 19.9 %collective-permute-start.1 = (f32[2,64,5,256]{3,1,2,0:T(8,128)}, f32[2,64,5,256]{3,1,2,0:T(8,128)}, u32[]{:S(2)}, u32[]{:S(2)}) collective-permute-start(f32[2,64,5,256]{3,1,2,0:T(8,128)} %copy.103), channel_id=1, source_target_pairs={{1,0},{2,1},{3,2},{4,3},{5,4},{6,5},{7,6},{8,7},{9,8},{10,9},{11,1... | collective-permute-start | bytes 1966088 | tf_op jit(solution)/shard_map/ppermute | solution.py:20
  41.2 27.4 %all-to-all-start = ((f32[2,1,294912]{2,1,0:T(1,128)}), f32[2,1,294912]{2,1,0:T(1,128)S(1)}, u32[]{:S(2)}, u32[]{:S(2)}) async-start(f32[2,1,294912]{2,1,0:T(1,128)} %reshape.70), calls=%async_computation | async-start | bytes 4718592 | tf_op jit(solution)/shard_map/all_to_all | solution.py:91
  99.4 9.1 %collective-permute-start.2 = (f32[2,128,18,5]{1,0,3,2:T(2,128)S(1)}, f32[2,128,18,5]{1,0,3,2:T(2,128)S(1)}, u32[]{:S(2)}, u32[]{:S(2)}) collective-permute-start(f32[2,128,18,5]{1,0,3,2:T(2,128)S(1)} %copy.77), channel_id=1, source_target_pairs={{0,16},{1,17},{2,18},{3,19},{4,20},{5,21},{6,22},{7,23},{8,24},{9,... | collective-permute-start | bytes 276488 | tf_op jit(solution)/shard_map/ppermute | solution.py:18
  104.0 6.4 %collective-permute-start.3 = (f32[2,128,18,5]{1,0,3,2:T(2,128)S(1)}, f32[2,128,18,5]{1,0,3,2:T(2,128)S(1)}, u32[]{:S(2)}, u32[]{:S(2)}) collective-permute-start(f32[2,128,18,5]{1,0,3,2:T(2,128)S(1)} %copy.78), channel_id=1, source_target_pairs={{16,0},{17,1},{18,2},{19,3},{20,4},{21,5},{22,6},{23,7},{24,8},{25... | collective-permute-start | bytes 276488 | tf_op jit(solution)/shard_map/ppermute | solution.py:20
  176.0 6.2 %copy-start.16 = (f32[1,128,18,138]{1,0,3,2:T(1,128)S(1)}, f32[1,128,18,138]{1,0,3,2:T(1,128)}, u32[]{:S(2)}) copy-start(f32[1,128,18,138]{1,0,3,2:T(1,128)} %fusion.59) | copy-start | bytes 3815428
  182.9 2.3 copy-start.29
  182.9 2.3 copy-start.30
  194.3 7.0 %copy-start.28 = (f32[1,123,18,138]{1,0,3,2:T(1,128)S(1)}, f32[1,123,18,138]{1,0,3,2:T(1,128)}, u32[]{:S(2)}) copy-start(f32[1,123,18,138]{1,0,3,2:T(1,128)} %get-tuple-element.203) | copy-start | bytes 3666388
  302.8 2.6 copy-start.15
  302.8 2.6 copy-start.37
  310.9 2.3 copy-start.10
  310.9 2.4 copy-start.32
  316.1 2.3 copy-start.9
  316.1 2.4 copy-start.31
  324.4 1.9 copy-start.4
  327.6 1.9 copy-start.2
  341.6 1.9 copy-start.4
  344.7 1.9 copy-start.2
  358.7 1.9 copy-start.4
  375.8 1.9 copy-start.4
  393.0 1.9 copy-start.4
  (49 other events, 73.2 us)
where the time goes:
time: 416 us; the launch traced here: 409 us
  other arithmetic  154 us (37%)
  local copies, waits for them, and re-layouts  145 us (35%)
  matrix products  58.9 us (14%)
  waiting for transfers between devices  36 us (9%)
  starting transfers between devices  13.6 us (3%)
    another operation x8, local copies, waits for them, and re-layouts, coherence(): sums = box_sum(jnp.stack([prod_re, prod_im]))  51.5 us
    add x8, other arithmetic, coherence(): prod_re = earlier[0] * later[0] + earlier[1] * later[1]  50.5 us
    dot_general x9, matrix products, box_sum(): jnp.einsum('...rc,kr->...kc', samples, row_table, precision=lax.Precision...  48.7 us
    sub x40, other arithmetic, apply_matrix(): back_im = coh_re * vector[1] - coh_im * vector[0]  39 us
    unnamed x71, local copies, waits for them, and re-layouts  27.1 us
    all_to_all x1, waiting for transfers between devices, regroup(): lax.all_to_all(samples, 'date', split_axis=3, concat_axis=1, tiled=True)  23 us
    another operation x8, other arithmetic, coherence(): sums = box_sum(jnp.stack([prod_re, prod_im]))  22.7 us
    reduce_sum x5, other arithmetic, apply_matrix(): meansq = jnp.mean(image[0] * image[0] + image[1] * image[1], axis=0)  20.3 us
  transfers between devices with their start and end apart: 5, of which 3 were waited for; matrix products, arithmetic and copies ran while one was open for 3% of the time, Pallas kernels for 0%

commit v1 on v0

--- a/solution.py
+++ b/solution.py
@@ -88,7 +88,10 @@
 
 
 def regroup(samples):
-    return lax.all_to_all(samples, "date", split_axis=3, concat_axis=1, tiled=True)
+    return jnp.concatenate(
+        lax.all_to_all(jnp.stack(jnp.split(samples, lax.axis_size("date"), axis=3)), "date", 0, 0),
+        axis=1,
+    )
 
 
 def add_row_rims(samples):

time: 416 us -> 376 us (0.904)
  local copies, waits for them, and re-layouts: 145 us -> 115 us
  other arithmetic: 154 us -> 141 us
    unnamed x71 -> x70, local copies, waits for them, and re-layouts: 27.1 us -> 11.4 us
    all_to_all x4 -> x1, local copies, waits for them, and re-layouts: 12 us -> 1.82 us  [regroup(): lax.all_to_all(jnp.stack(jnp.split(samples, lax.axis_size('date'), axis=3...]
    all_to_all x1 -> x0, other arithmetic: 9.05 us -> none  [regroup(): lax.all_to_all(samples, 'date', split_axis=3, concat_axis=1, tiled=True)]
    ppermute x2 -> x0, local copies, waits for them, and re-layouts: 7.13 us -> none  [the longest x1 3.6 us: extended_2(): lax.ppermute(tail, axis, [(i, (i + 1) % count) for i in range(ends)])]
    unnamed x1 -> x0, other arithmetic: 6.05 us -> none
  transfers between devices with their start and end apart: 5 -> 5, of which waited for: 3 -> 3; matrix products, arithmetic and copies ran while one was open for 3% -> 2% of each run, Pallas kernels for 0% -> 0%
where the time goes in v1:
time: 376 us; the launch traced here: 371 us
  other arithmetic  141 us (38%)
  local copies, waits for them, and re-layouts  115 us (31%)
  matrix products  58.9 us (16%)
  waiting for transfers between devices  40.1 us (11%)
  starting transfers between devices  14.7 us (4%)
    another operation x8, local copies, waits for them, and re-layouts, coherence(): sums = box_sum(jnp.stack([prod_re, prod_im]))  51.4 us
    add x8, other arithmetic, coherence(): prod_re = earlier[0] * later[0] + earlier[1] * later[1]  50.4 us
    dot_general x9, matrix products, box_sum(): jnp.einsum('...rc,kr->...kc', samples, row_table, precision=lax.Precision...  48.7 us
    sub x40, other arithmetic, apply_matrix(): back_im = coh_re * vector[1] - coh_im * vector[0]  38.8 us
    all_to_all x1, waiting for transfers between devices, regroup(): lax.all_to_all(jnp.stack(jnp.split(samples, lax.axis_size('date'), axis=3...  25.5 us
    another operation x8, other arithmetic, coherence(): sums = box_sum(jnp.stack([prod_re, prod_im]))  22.7 us
    reduce_sum x5, other arithmetic, apply_matrix(): meansq = jnp.mean(image[0] * image[0] + image[1] * image[1], axis=0)  20.3 us
    while x70, local copies, waits for them, and re-layouts  19.5 us
  transfers between devices with their start and end apart: 5, of which 3 were waited for; matrix products, arithmetic and copies ran while one was open for 2% of the time, Pallas kernels for 0%

profile of v1, /device:TPU:10, one launch (start us, length us, event | category | flops | bytes accessed | tf_op | source)
XLA Modules:
  0.0 371.2 jit_solution(7460842613589673557)
XLA Ops:
  7.9 13.1 %collective-permute-done = f32[2,64,5,256]{3,1,2,0:T(8,128)S(1)} collective-permute-done((f32[2,64,5,256]{3,1,2,0:T(8,128)S(1)}, f32[2,64,5,256]{3,1,2,0:T(8,128)S(1)}, u32[]{:S(2)}, u32[]{:S(2)}) %collective-permute-start) | collective-permute-done | bytes 655392 | tf_op jit(solution)/shard_map/ppermute | solution.py:18
  28.3 25.5 %all-to-all-done = f32[2,2,64,18,128]{4,2,3,1,0:T(8,128)} async-done(((f32[2,2,64,18,128]{4,2,3,1,0:T(8,128)}), f32[2,2,64,18,128]{4,2,3,1,0:T(8,128)}, u32[]{:S(2)}, u32[]{:S(2)}) %all-to-all-start) | async-done | bytes 2359328 | tf_op jit(solution)/shard_map/all_to_all | solution.py:92
  83.0 6.4 %multiply_add_fusion.8 = (f32[1,120,18,138]{1,0,3,2:T(1,128)}, f32[1,120,18,138]{1,0,3,2:T(1,128)}) fusion(f32[2,128,18,138]{1,0,3,2:T(2,128)S(1)} %pad_maximum_fusion), kind=kLoop, calls=%fused_computation.112 | loop fusion | flops 1788480 | bytes 7153920 | tf_op jit(solution)/shard_map/add | solution.py:52
  89.4 6.3 %multiply_add_fusion.11 = (f32[1,123,18,138]{1,0,3,2:T(1,128)}, f32[1,123,18,138]{1,0,3,2:T(1,128)}) fusion(f32[2,128,18,138]{1,0,3,2:T(2,128)S(1)} %pad_maximum_fusion), kind=kLoop, calls=%fused_computation.118 | loop fusion | flops 1833192 | bytes 7332768 | tf_op jit(solution)/shard_map/add | solution.py:52
  95.7 6.4 %multiply_add_fusion.10 = (f32[1,122,18,138]{1,0,3,2:T(1,128)}, f32[1,122,18,138]{1,0,3,2:T(1,128)}) fusion(f32[2,128,18,138]{1,0,3,2:T(2,128)S(1)} %pad_maximum_fusion), kind=kLoop, calls=%fused_computation.116 | loop fusion | flops 1818288 | bytes 7273152 | tf_op jit(solution)/shard_map/add | solution.py:52
  102.1 6.6 %multiply_add_fusion.13 = (f32[1,125,18,138]{1,0,3,2:T(1,128)}, f32[1,125,18,138]{1,0,3,2:T(1,128)}) fusion(f32[2,128,18,138]{1,0,3,2:T(2,128)S(1)} %pad_maximum_fusion), kind=kLoop, calls=%fused_computation.122 | loop fusion | flops 1863000 | bytes 7452000 | tf_op jit(solution)/shard_map/add | solution.py:52
  108.7 6.4 %multiply_add_fusion.12 = (f32[1,124,18,138]{1,0,3,2:T(1,128)}, f32[1,124,18,138]{1,0,3,2:T(1,128)}) fusion(f32[2,128,18,138]{1,0,3,2:T(2,128)S(1)} %pad_maximum_fusion), kind=kLoop, calls=%fused_computation.120 | loop fusion | flops 1848096 | bytes 7392384 | tf_op jit(solution)/shard_map/add | solution.py:52
  115.0 6.5 %multiply_add_fusion.15 = (f32[1,127,18,138]{1,0,3,2:T(1,128)}, f32[1,127,18,138]{1,0,3,2:T(1,128)}) fusion(f32[2,128,18,138]{1,0,3,2:T(2,128)S(1)} %pad_maximum_fusion), kind=kLoop, calls=%fused_computation.126 | loop fusion | flops 1892808 | bytes 7571232 | tf_op jit(solution)/shard_map/add | solution.py:52
  121.5 6.4 %multiply_add_fusion.14 = (f32[1,126,18,138]{1,0,3,2:T(1,128)}, f32[1,126,18,138]{1,0,3,2:T(1,128)}) fusion(f32[2,128,18,138]{1,0,3,2:T(2,128)S(1)} %pad_maximum_fusion), kind=kLoop, calls=%fused_computation.124 | loop fusion | flops 1877904 | bytes 7511616 | tf_op jit(solution)/shard_map/add | solution.py:52
  130.7 6.5 %copy.63 = f32[2,121,18,138]{3,2,1,0:T(8,128)} copy(f32[2,121,18,138]{1,0,3,2:T(2,128)S(1)} %pad_maximum_fusion.7) | data formatting | bytes 4809024 | tf_op jit(solution)/shard_map/stack | solution.py:54
  137.2 6.2 %fusion.91 = f32[8,2,121,138]{3,0,2,1:T(8,128)} fusion(f32[2,121,18,138]{3,2,1,0:T(8,128)} %copy.63), kind=kOutput, calls=%fused_computation.179 | convolution fusion | flops 57708864 | bytes 3473184 | tf_op jit(solution)/shard_map/...rc,kr->...kc/dot_general | solution.py:40
  149.3 6.5 %copy.65 = f32[2,120,18,138]{3,2,1,0:T(8,128)} copy(f32[2,120,18,138]{1,0,3,2:T(2,128)S(1)} %pad_maximum_fusion.8) | data formatting | bytes 4769280 | tf_op jit(solution)/shard_map/stack | solution.py:54
  155.8 6.1 %fusion.89 = f32[8,2,120,138]{3,0,2,1:T(8,128)} fusion(f32[2,120,18,138]{3,2,1,0:T(8,128)} %copy.65), kind=kOutput, calls=%fused_computation.177 | convolution fusion | flops 57231936 | bytes 3444480 | tf_op jit(solution)/shard_map/...rc,kr->...kc/dot_general | solution.py:40
  166.2 6.3 %copy.59 = f32[2,123,18,138]{3,2,1,0:T(8,128)} copy(f32[2,123,18,138]{1,0,3,2:T(2,128)S(1)} %pad_maximum_fusion.5) | data formatting | bytes 4888512 | tf_op jit(solution)/shard_map/stack | solution.py:54
  172.5 6.1 %fusion.95 = f32[8,2,123,138]{3,0,2,1:T(8,128)} fusion(f32[2,123,18,138]{3,2,1,0:T(8,128)} %copy.59), kind=kOutput, calls=%fused_computation.183 | convolution fusion | flops 58662720 | bytes 3530592 | tf_op jit(solution)/shard_map/...rc,kr->...kc/dot_general | solution.py:40
  183.3 6.4 %copy.61 = f32[2,122,18,138]{3,2,1,0:T(8,128)} copy(f32[2,122,18,138]{1,0,3,2:T(2,128)S(1)} %pad_maximum_fusion.6) | data formatting | bytes 4848768 | tf_op jit(solution)/shard_map/stack | solution.py:54
  200.4 6.3 %copy.55 = f32[2,125,18,138]{3,2,1,0:T(8,128)} copy(f32[2,125,18,138]{1,0,3,2:T(2,128)S(1)} %pad_maximum_fusion.3) | data formatting | bytes 4968000 | tf_op jit(solution)/shard_map/stack | solution.py:54
  206.7 6.2 %fusion.99 = f32[8,2,125,138]{3,0,2,1:T(8,128)} fusion(f32[2,125,18,138]{3,2,1,0:T(8,128)} %copy.55), kind=kOutput, calls=%fused_computation.187 | convolution fusion | flops 59616576 | bytes 3588000 | tf_op jit(solution)/shard_map/...rc,kr->...kc/dot_general | solution.py:40
  217.6 6.7 %copy.57 = f32[2,124,18,138]{3,2,1,0:T(8,128)} copy(f32[2,124,18,138]{1,0,3,2:T(2,128)S(1)} %pad_maximum_fusion.4) | data formatting | bytes 4928256 | tf_op jit(solution)/shard_map/stack | solution.py:54
  224.3 6.2 %fusion.97 = f32[8,2,124,138]{3,0,2,1:T(8,128)} fusion(f32[2,124,18,138]{3,2,1,0:T(8,128)} %copy.57), kind=kOutput, calls=%fused_computation.185 | convolution fusion | flops 59139648 | bytes 3559296 | tf_op jit(solution)/shard_map/...rc,kr->...kc/dot_general | solution.py:40
  235.2 6.3 %copy.49 = f32[2,127,18,138]{3,2,1,0:T(8,128)} copy(f32[2,127,18,138]{1,0,3,2:T(2,128)S(1)} %pad_maximum_fusion.1) | data formatting | bytes 5047488 | tf_op jit(solution)/shard_map/stack | solution.py:54
  241.5 6.3 %fusion.103 = f32[8,2,127,138]{3,0,2,1:T(8,128)} fusion(f32[2,127,18,138]{3,2,1,0:T(8,128)} %copy.49), kind=kOutput, calls=%fused_computation.191 | convolution fusion | flops 60570432 | bytes 3645408 | tf_op jit(solution)/shard_map/...rc,kr->...kc/dot_general | solution.py:40
  252.6 6.5 %copy.53 = f32[2,126,18,138]{3,2,1,0:T(8,128)} copy(f32[2,126,18,138]{1,0,3,2:T(2,128)S(1)} %pad_maximum_fusion.2) | data formatting | bytes 5007744 | tf_op jit(solution)/shard_map/stack | solution.py:54
  284.4 85.6 %while.12 = (s32[]{:T(128)}, f32[2,128,8,128]{3,2,1,0:T(8,128)S(1)}, f32[1,2,128,8,128]{4,3,2,1,0:T(8,128)}, f32[1,2,128,8,128]{4,3,2,1,0:T(8,128)}, f32[1,2,128...) while((s32[]{:T(128)}, ...), condition=%wide.region_2.3_spmd, body=%wide.region_0.2_spmd.sunk | while | flops 17605632 | bytes 115360056 | solution.py:87
  (329 shorter events, 197.6 us)
Async XLA Ops:
  1.7 6.1 %copy-start.39 = (s32[128,8]{0,1:T(8,128)S(1)}, s32[128,8]{0,1:T(8,128)}, u32[]{:S(2)}) copy-start(s32[128,8]{0,1:T(8,128)} %param.5) | copy-start | bytes 12292
  1.7 19.3 %copy-start.8 = (f32[2,64,8,256]{3,2,1,0:T(8,128)S(1)}, f32[2,64,8,256]{3,2,1,0:T(8,128)}, u32[]{:S(2)}) copy-start(f32[2,64,8,256]{3,2,1,0:T(8,128)} %param.4) | copy-start | bytes 3145732
  1.9 19.1 %collective-permute-start = (f32[2,64,5,256]{3,1,2,0:T(8,128)S(1)}, f32[2,64,5,256]{3,1,2,0:T(8,128)S(1)}, u32[]{:S(2)}, u32[]{:S(2)}) collective-permute-start(f32[2,64,5,256]{3,1,2,0:T(8,128)S(1)} %copy.79), channel_id=1, source_target_pairs={{0,1},{1,2},{2,3},{3,4},{4,5},{5,6},{6,7},{7,8},{8,9},{9,10},{10,1... | collective-permute-start | bytes 1966088 | tf_op jit(solution)/shard_map/ppermute | solution.py:18
  4.2 17.2 %collective-permute-start.1 = (f32[2,64,5,256]{3,1,2,0:T(8,128)S(1)}, f32[2,64,5,256]{3,1,2,0:T(8,128)S(1)}, u32[]{:S(2)}, u32[]{:S(2)}) collective-permute-start(f32[2,64,5,256]{3,1,2,0:T(8,128)S(1)} %copy.80), channel_id=1, source_target_pairs={{1,0},{2,1},{3,2},{4,3},{5,4},{6,5},{7,6},{8,7},{9,8},{10,9},{11,1... | collective-permute-start | bytes 1966088 | tf_op jit(solution)/shard_map/ppermute | solution.py:20
  23.3 30.5 %all-to-all-start = ((f32[2,2,64,18,128]{4,2,3,1,0:T(8,128)}), f32[2,2,64,18,128]{4,2,3,1,0:T(8,128)}, u32[]{:S(2)}, u32[]{:S(2)}) async-start(f32[2,2,64,18,128]{4,2,3,1,0:T(8,128)} %pad_maximum_fusion.9), calls=%async_computation | async-start | bytes 4718592 | tf_op jit(solution)/shard_map/all_to_all | solution.py:92
  61.0 9.5 %collective-permute-start.2 = (f32[2,128,18,5]{1,0,3,2:T(2,128)S(1)}, f32[2,128,18,5]{1,0,3,2:T(2,128)S(1)}, u32[]{:S(2)}, u32[]{:S(2)}) collective-permute-start(f32[2,128,18,5]{1,0,3,2:T(2,128)S(1)} %copy.46), channel_id=1, source_target_pairs={{0,16},{1,17},{2,18},{3,19},{4,20},{5,21},{6,22},{7,23},{8,24},{9,... | collective-permute-start | bytes 276488 | tf_op jit(solution)/shard_map/ppermute | solution.py:18
  65.6 6.4 %collective-permute-start.3 = (f32[2,128,18,5]{1,0,3,2:T(2,128)S(1)}, f32[2,128,18,5]{1,0,3,2:T(2,128)S(1)}, u32[]{:S(2)}, u32[]{:S(2)}) collective-permute-start(f32[2,128,18,5]{1,0,3,2:T(2,128)S(1)} %copy.47), channel_id=1, source_target_pairs={{16,0},{17,1},{18,2},{19,3},{20,4},{21,5},{22,6},{23,7},{24,8},{25... | collective-permute-start | bytes 276488 | tf_op jit(solution)/shard_map/ppermute | solution.py:20
  137.2 6.2 %copy-start.16 = (f32[1,128,18,138]{1,0,3,2:T(1,128)S(1)}, f32[1,128,18,138]{1,0,3,2:T(1,128)}, u32[]{:S(2)}) copy-start(f32[1,128,18,138]{1,0,3,2:T(1,128)} %fusion.59) | copy-start | bytes 3815428
  144.1 2.3 copy-start.29
  144.1 2.3 copy-start.30
  155.8 7.0 %copy-start.28 = (f32[1,123,18,138]{1,0,3,2:T(1,128)S(1)}, f32[1,123,18,138]{1,0,3,2:T(1,128)}, u32[]{:S(2)}) copy-start(f32[1,123,18,138]{1,0,3,2:T(1,128)} %get-tuple-element.203) | copy-start | bytes 3666388
  272.7 2.3 copy-start.10
  272.7 2.4 copy-start.32
  277.9 2.3 copy-start.9
  277.9 2.4 copy-start.31
  286.2 1.9 copy-start.4
  289.4 1.9 copy-start.2
  303.3 1.9 copy-start.4
  306.5 1.9 copy-start.2
  320.5 1.9 copy-start.4
  323.6 1.9 copy-start.2
  337.6 1.9 copy-start.4
  340.7 1.9 copy-start.2
  354.7 1.9 copy-start.4
  (49 other events, 72.6 us)
